TPU v7x, 32 devices: a whole 2x2x4 slice. The times are simulated.
32 devices in a mesh: loop: 4 (over x, core), grp: 8 (over z, y).
Axes of the slice: x: 2, y: 2, z: 4, core: 2. Of those that a mesh axis runs over, the one named last changes fastest.
Arguments:
- basis: bfloat16 [24576, 256], P(('loop', 'grp')), may hold values from -6 to 6
- stiffness: bfloat16 [384, 16, 4096], P(('loop', 'grp')), may hold values from -0.1875 to 0.1875
- mass: bfloat16 [384, 16, 4096], P(('loop', 'grp')), may hold values from -0.1875 to 0.1875
- col_index: int32 [384, 16], P(('loop', 'grp')), may hold values from 0 to 11
- live_counts: int32 [384], P(('loop', 'grp')), may hold values from 1 to 16, as said below
Outputs:
- stiff_basis: bfloat16 [24576, 256], P(('loop', 'grp'))
- mass_basis: bfloat16 [24576, 256], P(('loop', 'grp'))
- stiff_gram: float32 [256, 256], replicated
- mass_gram: float32 [256, 256], replicated
Inputs may be any that keep to these rules, and one draw needn't show every extreme that they name: `live_counts`: every block row keeps at least one block; some block row uses all 16 and some only one.
All inputs are finite; a program needn't handle non-finite values.
Results may differ from a plain program's by a relative error of at most 0.0029.
Values may be sent and summed in bfloat16 or wider, within the bound.
A program may use at most 64 MiB of HBM per device.

v0:
```python
import jax
import jax.numpy as jnp
from jax import lax
from jax.sharding import PartitionSpec as P

BS = 64
NB = 16
panel_spans = ((0, 0, 6), (1, 6, 3), (-1, 9, 3), (2, 12, 2), (-2, 14, 2))


def shifted(block, axis, distance):
    devices = range(lax.axis_size(axis))
    route = [((i - distance) % len(devices), i) for i in devices]
    return lax.ppermute(block, axis, route)


def on_device(basis, stiffness, mass, col_index, live_counts):
    rows_dev = stiffness.shape[0]
    width = basis.shape[1]
    kb = stiffness.reshape(rows_dev, NB, BS, BS)
    mb = mass.reshape(rows_dev, NB, BS, BS)
    slot_ids = jnp.arange(NB, dtype=jnp.int32)
    live_grid = slot_ids[None, :] < live_counts[:, None]
    panels = {
        0: basis,
        1: shifted(basis, "loop", -1),
        -1: shifted(basis, "loop", 1),
        2: shifted(basis, "loop", -2),
        -2: shifted(basis, "loop", 2),
    }
    zeros_acc = jnp.zeros((rows_dev, BS, width), jnp.float32)
    accs = (zeros_acc, zeros_acc)
    for shift_by, first, count in panel_spans:
        blocks = panels[shift_by].reshape(rows_dev, BS, width)
        chosen = col_index[:, first : first + count]
        alive = live_grid[:, first : first + count]
        picked = blocks[chosen]
        picked = jnp.where(alive[:, :, None, None], picked, jnp.zeros_like(picked))
        kadd = jnp.einsum(
            "rjab,rjbc->rac",
            kb[:, first : first + count],
            picked,
            preferred_element_type=jnp.float32,
        )
        madd = jnp.einsum(
            "rjab,rjbc->rac",
            mb[:, first : first + count],
            picked,
            preferred_element_type=jnp.float32,
        )
        accs = (accs[0] + kadd, accs[1] + madd)
    kacc, macc = accs
    stiff_basis = kacc.reshape(rows_dev * BS, width).astype(jnp.bfloat16)
    mass_basis = macc.reshape(rows_dev * BS, width).astype(jnp.bfloat16)
    contract = (((0,), (0,)), ((), ()))
    kterm = lax.dot_general(basis, stiff_basis, contract, preferred_element_type=jnp.float32)
    mterm = lax.dot_general(basis, mass_basis, contract, preferred_element_type=jnp.float32)
    kgram, mgram = lax.psum((kterm, mterm), ("loop", "grp"))
    total_dofs = basis.shape[0] * lax.axis_size("loop") * lax.axis_size("grp")
    factor = jnp.float32(1.0) / jnp.sqrt(jnp.float32(total_dofs))
    return (stiff_basis, mass_basis, kgram * factor, mgram * factor)


def solution(mesh):
    in_specs = (
        P(("loop", "grp"), None),
        P(("loop", "grp"), None, None),
        P(("loop", "grp"), None, None),
        P(("loop", "grp"), None),
        P(("loop", "grp")),
    )
    out_specs = (P(("loop", "grp"), None), P(("loop", "grp"), None), P(), P())
    return jax.shard_map(
        on_device, mesh=mesh, in_specs=in_specs, out_specs=out_specs, check_vma=False
    )
```

profile of v0, /device:TPU:0, one launch (start us, length us, event | category | flops | bytes accessed | tf_op | source)
XLA Modules:
  0.0 197.9 jit_solution(3938690956162846545)
XLA Ops:
  7.7 2.0 %collective-permute-start = (bf16[768,256]{1,0:T(8,128)(2,1)}, bf16[768,256]{1,0:T(8,128)(2,1)}, u32[]{:S(2)}, u32[]{:S(2)}) collective-permute-start(bf16[768,256]{1,0:T(8,128)(2,1)} %param.5), channel_id=1, source_target_pairs={{8,0},{16,8},{24,16},{0,24},{9,1},{17,9},{25,17},{1,25},{10,2},{18... | collective-permute-start | bytes 1179656 | tf_op jit(solution)/shard_map/ppermute | solution.py:14
  9.7 2.2 %collective-permute-start.2 = (bf16[768,256]{1,0:T(8,128)(2,1)}, bf16[768,256]{1,0:T(8,128)(2,1)}, u32[]{:S(2)}, u32[]{:S(2)}) collective-permute-start(bf16[768,256]{1,0:T(8,128)(2,1)} %param.5), channel_id=1, source_target_pairs={{16,0},{24,8},{0,16},{8,24},{17,1},{25,9},{1,17},{9,25},{18,2},{26... | collective-permute-start | bytes 1179656 | tf_op jit(solution)/shard_map/ppermute | solution.py:14
  11.9 0.8 compare_select_fusion.3
  15.5 0.8 compare_select_fusion.1
  16.4 4.3 %reshape.42 = bf16[12,16,64,64]{3,2,1,0:T(8,128)(2,1)S(1)} reshape(bf16[12,16,4096]{2,1,0:T(8,128)(2,1)} %param.7) | data formatting | bytes 3145728 | tf_op jit(solution)/shard_map/reshape | solution.py:21
  22.4 5.5 %reshape.38 = bf16[12,16,64,64]{3,2,1,0:T(8,128)(2,1)} reshape(bf16[12,16,4096]{2,1,0:T(8,128)(2,1)} %param.6) | data formatting | bytes 3145728 | tf_op jit(solution)/shard_map/reshape | solution.py:20
  27.9 2.4 %gather_fusion = bf16[72,64,256]{2,1,0:T(8,128)(2,1)} fusion(bf16[12,64,256]{2,1,0:T(8,128)(2,1)S(1)} %bitcast.84, s32[1024]{0:T(1024)S(1)} %pad_clamp_fusion.4), kind=kCustom, calls=%fused_computation | custom fusion | bytes 4718880 | tf_op jit(solution)/shard_map/gather | solution.py:37
  30.3 3.3 %fusion.2 = f32[12,256,64]{1,2,0:T(8,128)} fusion(bf16[12,16,64,64]{3,2,1,0:T(8,128)(2,1)S(1)} %reshape.42, bf16[12,6,64,256]{3,2,1,0:T(8,128)(2,1)} %bitcast.91, pred[12,6]{1,0:T(8,128)(4,1)S(1)} %bitcast.99), kind=kOutput, calls=%fused_computation.8 | convolution fusion | flops 152174592 | bytes 4718664 | tf_op jit(solution)/shard_map/rjab,rjbc->rac/dot_general | solution.py:45
  33.6 1.5 fusion.3
  35.2 2.6 %gather_fusion.4 = bf16[24,64,256]{2,1,0:T(8,128)(2,1)} fusion(bf16[12,64,256]{2,1,0:T(8,128)(2,1)} %bitcast.12, s32[1024]{0:T(1024)S(1)} %copy-done.15), kind=kCustom, calls=%fused_computation.4 | custom fusion | bytes 1572960 | tf_op jit(solution)/shard_map/gather | solution.py:37
  37.7 2.6 %gather_fusion.3 = bf16[24,64,256]{2,1,0:T(8,128)(2,1)} fusion(bf16[12,64,256]{2,1,0:T(8,128)(2,1)} %bitcast.12, s32[1024]{0:T(1024)} %pad_clamp_fusion.1), kind=kCustom, calls=%fused_computation.3 | custom fusion | bytes 1572960 | tf_op jit(solution)/shard_map/gather | solution.py:37
  40.4 2.7 %gather_fusion.2 = bf16[36,64,256]{2,1,0:T(8,128)(2,1)} fusion(bf16[12,64,256]{2,1,0:T(8,128)(2,1)} %bitcast.8, s32[1024]{0:T(1024)S(1)} %pad_clamp_fusion.2), kind=kCustom, calls=%fused_computation.2 | custom fusion | bytes 2359440 | tf_op jit(solution)/shard_map/gather | solution.py:37
  43.1 2.7 %convolution_bitcast_fusion.4 = f32[12,256,64]{1,2,0:T(8,128)} fusion(bf16[12,16,64,64]{3,2,1,0:T(8,128)(2,1)S(1)} %reshape.42, bf16[12,3,64,256]{3,2,1,0:T(8,128)(2,1)} %bitcast.97, pred[12,3]{1,0:T(8,128)(4,1)S(1)} %copy-done.19), kind=kOutput, calls=%fused_computation.14 | convolution fusion | flops 76087296 | bytes 3538980 | tf_op jit(solution)/shard_map/rjab,rjbc->rac/dot_general | solution.py:45
  45.8 1.3 convolution_bitcast_fusion
  47.1 1.2 convolution_bitcast_fusion.2
  48.3 1.3 convolution_bitcast_fusion.6
  49.6 2.7 %gather_fusion.1 = bf16[36,64,256]{2,1,0:T(8,128)(2,1)} fusion(bf16[12,64,256]{2,1,0:T(8,128)(2,1)} %bitcast.4, s32[1024]{0:T(1024)S(1)} %pad_clamp_fusion.3), kind=kCustom, calls=%fused_computation.1 | custom fusion | bytes 2359440 | tf_op jit(solution)/shard_map/gather | solution.py:37
  52.4 2.3 %fusion.11 = f32[12,256,64]{1,2,0:T(8,128)S(1)} fusion(f32[12,256,64]{1,2,0:T(8,128)} %convolution_bitcast_fusion.4, f32[12,256,64]{1,2,0:T(8,128)} %fusion.2, bf16[12,16,64,64]{3,2,1,0:T(8,128)(2,1)S(1)} %reshape.42, bf16[12,3,64,256]{3,2,1,0:T(8,128)(2,1)} %bitcast.85, pred[12,3]{1,0:T(8,128)(4,1)S(1)} %copy-done.17), kind=kOutput, calls=%fused_computation.25 | convolution fusion | flops 76480512 | bytes 5111844 | tf_op jit(solution)/shard_map/rjab,rjbc->rac/dot_general | solution.py:45
  55.1 1.0 convolution_bitcast_fusion.8
  58.7 1.0 convolution_bitcast_fusion.9
  59.7 128.6 %all-reduce.3.cloned.1.call-done = (f32[256,256]{0,1:T(8,128)}, f32[256,256]{0,1:T(8,128)}) async-done(((f32[256,256]{0,1:T(8,128)}, f32[256,256]{0,1:T(8,128)}), (f32[256,256]{0,1:T(8,128)}, f32[256,256]{0,1:T(8,128)})) %all-reduce.3.cloned.1.call-update) | async-done | bytes 524304 | tf_op jit(solution)/shard_map/psum | solution.py:58
  188.3 1.1 broadcast_multiply_fusion
  189.4 0.8 copy.11
  190.2 0.8 copy.12
  (63 shorter events, 7.9 us)
Async XLA Ops:
  7.2 181.1 %all-reduce.3.cloned.1.call-start = ((), (), s32[]{:S(2)}) async-start(), calls=%async_computation | async-start | bytes 1048576 | tf_op jit(solution)/shard_map/psum | solution.py:58
  7.2 33.1 %collective-permute-start.1 = (bf16[768,256]{1,0:T(8,128)(2,1)}, bf16[768,256]{1,0:T(8,128)(2,1)}, u32[]{:S(2)}, u32[]{:S(2)}) collective-permute-start(bf16[768,256]{1,0:T(8,128)(2,1)} %param.5), channel_id=1, source_target_pairs={{24,0},{0,8},{8,16},{16,24},{25,1},{1,9},{9,17},{17,25},{26,2},{2,... | collective-permute-start | bytes 1179656 | tf_op jit(solution)/shard_map/ppermute | solution.py:14
  7.7 41.9 %collective-permute-start = (bf16[768,256]{1,0:T(8,128)(2,1)}, bf16[768,256]{1,0:T(8,128)(2,1)}, u32[]{:S(2)}, u32[]{:S(2)}) collective-permute-start(bf16[768,256]{1,0:T(8,128)(2,1)} %param.5), channel_id=1, source_target_pairs={{8,0},{16,8},{24,16},{0,24},{9,1},{17,9},{25,17},{1,25},{10,2},{18... | collective-permute-start | bytes 1179656 | tf_op jit(solution)/shard_map/ppermute | solution.py:14
  9.7 25.5 %collective-permute-start.2 = (bf16[768,256]{1,0:T(8,128)(2,1)}, bf16[768,256]{1,0:T(8,128)(2,1)}, u32[]{:S(2)}, u32[]{:S(2)}) collective-permute-start(bf16[768,256]{1,0:T(8,128)(2,1)} %param.5), channel_id=1, source_target_pairs={{16,0},{24,8},{0,16},{8,24},{17,1},{25,9},{1,17},{9,25},{18,2},{26... | collective-permute-start | bytes 1179656 | tf_op jit(solution)/shard_map/ppermute | solution.py:14
  22.4 5.5 %copy-start = (bf16[768,256]{1,0:T(8,128)(2,1)S(1)}, bf16[768,256]{1,0:T(8,128)(2,1)}, u32[]{:S(2)}) copy-start(bf16[768,256]{1,0:T(8,128)(2,1)} %param.5) | copy-start | bytes 1179652
  30.3 3.3 %copy-start.1 = (bf16[12,16,64,64]{3,2,1,0:T(8,128)(2,1)S(1)}, bf16[12,16,64,64]{3,2,1,0:T(8,128)(2,1)}, u32[]{:S(2)}) copy-start(bf16[12,16,64,64]{3,2,1,0:T(8,128)(2,1)} %reshape.38) | copy-start | bytes 4718596
  30.3 3.3 %copy-start.9 = (bf16[72,64,256]{2,1,0:T(8,128)(2,1)S(1)}, bf16[72,64,256]{2,1,0:T(8,128)(2,1)}, u32[]{:S(2)}) copy-start(bf16[72,64,256]{2,1,0:T(8,128)(2,1)} %gather_fusion) | copy-start | bytes 7077892
  33.6 1.5 copy-start.15
  37.7 5.4 %copy-start.19 = (pred[12,3]{1,0:T(8,128)(4,1)S(1)}, pred[12,3]{1,0:T(8,128)(4,1)}, u32[]{:S(2)}) copy-start(pred[12,3]{1,0:T(8,128)(4,1)} %get-tuple-element.21) | copy-start | bytes 112
  40.4 5.5 %copy-start.18 = (pred[12,2]{1,0:T(8,128)(4,1)S(1)}, pred[12,2]{1,0:T(8,128)(4,1)}, u32[]{:S(2)}) copy-start(pred[12,2]{1,0:T(8,128)(4,1)} %get-tuple-element.19) | copy-start | bytes 76
  43.1 2.7 %copy-start.6 = (bf16[24,64,256]{2,1,0:T(8,128)(2,1)S(1)}, bf16[24,64,256]{2,1,0:T(8,128)(2,1)}, u32[]{:S(2)}) copy-start(bf16[24,64,256]{2,1,0:T(8,128)(2,1)} %gather_fusion.4) | copy-start | bytes 2359300
  43.1 4.0 %copy-start.2 = (bf16[12,16,64,64]{3,2,1,0:T(8,128)(2,1)S(1)}, bf16[12,16,64,64]{3,2,1,0:T(8,128)(2,1)}, u32[]{:S(2)}) copy-start(bf16[12,16,64,64]{3,2,1,0:T(8,128)(2,1)} %reshape.38) | copy-start | bytes 4718596
  45.8 2.5 %copy-start.12 = (bf16[36,64,256]{2,1,0:T(8,128)(2,1)S(1)}, bf16[36,64,256]{2,1,0:T(8,128)(2,1)}, u32[]{:S(2)}) copy-start(bf16[36,64,256]{2,1,0:T(8,128)(2,1)} %gather_fusion.2) | copy-start | bytes 3538948
  48.3 4.0 %copy-start.17 = (pred[12,3]{1,0:T(8,128)(4,1)S(1)}, pred[12,3]{1,0:T(8,128)(4,1)}, u32[]{:S(2)}) copy-start(pred[12,3]{1,0:T(8,128)(4,1)} %get-tuple-element.20) | copy-start | bytes 112
  52.4 2.3 %copy-start.5 = (bf16[24,64,256]{2,1,0:T(8,128)(2,1)S(1)}, bf16[24,64,256]{2,1,0:T(8,128)(2,1)}, u32[]{:S(2)}) copy-start(bf16[24,64,256]{2,1,0:T(8,128)(2,1)} %gather_fusion.3) | copy-start | bytes 2359300
  52.4 2.3 %copy-start.8 = (f32[12,256,64]{1,2,0:T(8,128)S(1)}, f32[12,256,64]{1,2,0:T(8,128)}, u32[]{:S(2)}) copy-start(f32[12,256,64]{1,2,0:T(8,128)} %convolution_bitcast_fusion) | copy-start | bytes 2359300
  52.4 2.4 %copy-start.16 = (pred[12,2]{1,0:T(8,128)(4,1)S(1)}, pred[12,2]{1,0:T(8,128)(4,1)}, u32[]{:S(2)}) copy-start(pred[12,2]{1,0:T(8,128)(4,1)} %get-tuple-element.18) | copy-start | bytes 76
  52.4 3.7 %copy-start.13 = (f32[12,256,64]{1,2,0:T(8,128)S(1)}, f32[12,256,64]{1,2,0:T(8,128)}, u32[]{:S(2)}) copy-start(f32[12,256,64]{1,2,0:T(8,128)} %fusion.3) | copy-start | bytes 2359300
  52.4 3.7 %copy-start.14 = (f32[12,256,64]{1,2,0:T(8,128)S(1)}, f32[12,256,64]{1,2,0:T(8,128)}, u32[]{:S(2)}) copy-start(f32[12,256,64]{1,2,0:T(8,128)} %convolution_bitcast_fusion.6) | copy-start | bytes 2359300
  54.7 2.2 %copy-start.3 = (bf16[12,16,64,64]{3,2,1,0:T(8,128)(2,1)S(1)}, bf16[12,16,64,64]{3,2,1,0:T(8,128)(2,1)}, u32[]{:S(2)}) copy-start(bf16[12,16,64,64]{3,2,1,0:T(8,128)(2,1)} %reshape.38) | copy-start | bytes 4718596
  54.7 2.5 %copy-start.4 = (bf16[36,64,256]{2,1,0:T(8,128)(2,1)S(1)}, bf16[36,64,256]{2,1,0:T(8,128)(2,1)}, u32[]{:S(2)}) copy-start(bf16[36,64,256]{2,1,0:T(8,128)(2,1)} %gather_fusion.1) | copy-start | bytes 3538948
  55.1 2.6 %copy-start.10 = (bf16[12,256,64]{1,2,0:T(8,128)(2,1)}, bf16[12,256,64]{1,2,0:T(8,128)(2,1)S(1)}, u32[]{:S(2)}) copy-start(bf16[12,256,64]{1,2,0:T(8,128)(2,1)S(1)} %fusion.12) | copy-start | bytes 1179652
  57.2 1.1 copy-start.7
  58.7 132.4 %copy-start.11 = (bf16[12,256,64]{1,2,0:T(8,128)(2,1)}, bf16[12,256,64]{1,2,0:T(8,128)(2,1)S(1)}, u32[]{:S(2)}) copy-start(bf16[12,256,64]{1,2,0:T(8,128)(2,1)S(1)} %fusion.13) | copy-start | bytes 1179652
Sparse Core Ops, SparseCore 0:
  59.8 128.3 all-reduce.2
where the time goes:
time: 198 us
  waiting for transfers between devices  129 us (65%)
  local copies, waits for them, and re-layouts  28.2 us (14%)
  matrix products  16.7 us (8%)
  between operations  14.2 us (7%)
  other arithmetic  5.42 us (3%)
  starting transfers between devices  4.77 us (2%)
    psum x1, waiting for transfers between devices, on_device(): kgram, mgram = lax.psum((kterm, mterm), ('loop', 'grp'))  129 us
    gather x5, local copies, waits for them, and re-layouts, on_device(): picked = blocks[chosen]  13 us
    dot_general x5, matrix products, on_device(): jnp.einsum('rjab,rjbc->rac', mb[:, first:first + count], picked, preferre...  9.93 us
    reshape x1, local copies, waits for them, and re-layouts, on_device(): kb = stiffness.reshape(rows_dev, NB, BS, BS)  5.54 us
    dot_general x5, matrix products, on_device(): jnp.einsum('rjab,rjbc->rac', kb[:, first:first + count], picked, preferre...  4.76 us
    ppermute x3, starting transfers between devices, shifted(): return lax.ppermute(block, axis, route)  4.74 us
    reshape x1, local copies, waits for them, and re-layouts, on_device(): mb = mass.reshape(rows_dev, NB, BS, BS)  4.31 us
  transfers between devices with their start and end apart: 4, of which 1 were waited for; matrix products, arithmetic and copies ran while one was open for 19% of the time, Pallas kernels for 0%

commit v1 on v0

--- a/solution.py
+++ b/solution.py
@@ -6,6 +6,11 @@
 BS = 64
 NB = 16
 panel_spans = ((0, 0, 6), (1, 6, 3), (-1, 9, 3), (2, 12, 2), (-2, 14, 2))
+
+
+def one_after_other(array, one, other):
+    inner = lax.psum(array, one)
+    return lax.psum(inner, other)
 
 
 def shifted(block, axis, distance):
@@ -55,7 +60,7 @@
     contract = (((0,), (0,)), ((), ()))
     kterm = lax.dot_general(basis, stiff_basis, contract, preferred_element_type=jnp.float32)
     mterm = lax.dot_general(basis, mass_basis, contract, preferred_element_type=jnp.float32)
-    kgram, mgram = lax.psum((kterm, mterm), ("loop", "grp"))
+    kgram, mgram = one_after_other((kterm, mterm), "grp", "loop")
     total_dofs = basis.shape[0] * lax.axis_size("loop") * lax.axis_size("grp")
     factor = jnp.float32(1.0) / jnp.sqrt(jnp.float32(total_dofs))
     return (stiff_basis, mass_basis, kgram * factor, mgram * factor)

time: 198 us -> 178 us (0.90)
  waiting for transfers between devices: 129 us -> 108 us
    psum x1 -> x2, waiting for transfers between devices: 129 us -> 108 us  [the longest x1 73 us: one_after_other(): inner = lax.psum(array, one)]
  transfers between devices with their start and end apart: 4 -> 5, of which waited for: 1 -> 2; matrix products, arithmetic and copies ran while one was open for 19% -> 21% of each run, Pallas kernels for 0% -> 0%
where the time goes in v1:
time: 178 us; the launch traced here: 177 us
  waiting for transfers between devices  108 us (61%)
  local copies, waits for them, and re-layouts  28.2 us (16%)
  matrix products  16.8 us (9%)
  between operations  14.2 us (8%)
  other arithmetic  5.42 us (3%)
  starting transfers between devices  4.81 us (3%)
    psum x1, waiting for transfers between devices, one_after_other(): inner = lax.psum(array, one)  73 us
    psum x1, waiting for transfers between devices, one_after_other(): return lax.psum(inner, other)  34.9 us
    gather x5, local copies, waits for them, and re-layouts, on_device(): picked = blocks[chosen]  13 us
    dot_general x5, matrix products, on_device(): jnp.einsum('rjab,rjbc->rac', mb[:, first:first + count], picked, preferre...  9.95 us
    reshape x1, local copies, waits for them, and re-layouts, on_device(): kb = stiffness.reshape(rows_dev, NB, BS, BS)  5.55 us
    dot_general x5, matrix products, on_device(): jnp.einsum('rjab,rjbc->rac', kb[:, first:first + count], picked, preferre...  4.8 us
    ppermute x3, starting transfers between devices, shifted(): return lax.ppermute(block, axis, route)  4.74 us
    reshape x1, local copies, waits for them, and re-layouts, on_device(): mb = mass.reshape(rows_dev, NB, BS, BS)  4.31 us
  transfers between devices with their start and end apart: 5, of which 2 were waited for; matrix products, arithmetic and copies ran while one was open for 21% of the time, Pallas kernels for 0%

profile of v1, /device:TPU:0, one launch (start us, length us, event | category | flops | bytes accessed | tf_op | source)
XLA Modules:
  0.0 177.4 jit_solution(12531716884711763628)
XLA Ops:
  7.7 2.0 %collective-permute-start = (bf16[768,256]{1,0:T(8,128)(2,1)}, bf16[768,256]{1,0:T(8,128)(2,1)}, u32[]{:S(2)}, u32[]{:S(2)}) collective-permute-start(bf16[768,256]{1,0:T(8,128)(2,1)} %param.5), channel_id=1, source_target_pairs={{8,0},{16,8},{24,16},{0,24},{9,1},{17,9},{25,17},{1,25},{10,2},{18... | collective-permute-start | bytes 1179656 | tf_op jit(solution)/shard_map/ppermute | solution.py:19
  9.7 2.2 %collective-permute-start.2 = (bf16[768,256]{1,0:T(8,128)(2,1)}, bf16[768,256]{1,0:T(8,128)(2,1)}, u32[]{:S(2)}, u32[]{:S(2)}) collective-permute-start(bf16[768,256]{1,0:T(8,128)(2,1)} %param.5), channel_id=1, source_target_pairs={{16,0},{24,8},{0,16},{8,24},{17,1},{25,9},{1,17},{9,25},{18,2},{26... | collective-permute-start | bytes 1179656 | tf_op jit(solution)/shard_map/ppermute | solution.py:19
  11.9 0.8 compare_select_fusion.3
  15.5 0.8 compare_select_fusion.1
  16.4 4.3 %reshape.42 = bf16[12,16,64,64]{3,2,1,0:T(8,128)(2,1)S(1)} reshape(bf16[12,16,4096]{2,1,0:T(8,128)(2,1)} %param.7) | data formatting | bytes 3145728 | tf_op jit(solution)/shard_map/reshape | solution.py:26
  22.4 5.5 %reshape.38 = bf16[12,16,64,64]{3,2,1,0:T(8,128)(2,1)} reshape(bf16[12,16,4096]{2,1,0:T(8,128)(2,1)} %param.6) | data formatting | bytes 3145728 | tf_op jit(solution)/shard_map/reshape | solution.py:25
  27.9 2.4 %gather_fusion = bf16[72,64,256]{2,1,0:T(8,128)(2,1)} fusion(bf16[12,64,256]{2,1,0:T(8,128)(2,1)S(1)} %bitcast.84, s32[1024]{0:T(1024)S(1)} %pad_clamp_fusion.4), kind=kCustom, calls=%fused_computation | custom fusion | bytes 4718880 | tf_op jit(solution)/shard_map/gather | solution.py:42
  30.3 3.4 %fusion.2 = f32[12,256,64]{1,2,0:T(8,128)} fusion(bf16[12,16,64,64]{3,2,1,0:T(8,128)(2,1)S(1)} %reshape.42, bf16[12,6,64,256]{3,2,1,0:T(8,128)(2,1)} %bitcast.91, pred[12,6]{1,0:T(8,128)(4,1)S(1)} %bitcast.99), kind=kOutput, calls=%fused_computation.8 | convolution fusion | flops 152174592 | bytes 4718664 | tf_op jit(solution)/shard_map/rjab,rjbc->rac/dot_general | solution.py:50
  33.7 1.5 fusion.3
  35.2 2.6 %gather_fusion.4 = bf16[24,64,256]{2,1,0:T(8,128)(2,1)} fusion(bf16[12,64,256]{2,1,0:T(8,128)(2,1)} %bitcast.12, s32[1024]{0:T(1024)S(1)} %copy-done.15), kind=kCustom, calls=%fused_computation.4 | custom fusion | bytes 1572960 | tf_op jit(solution)/shard_map/gather | solution.py:42
  37.8 2.6 %gather_fusion.3 = bf16[24,64,256]{2,1,0:T(8,128)(2,1)} fusion(bf16[12,64,256]{2,1,0:T(8,128)(2,1)} %bitcast.12, s32[1024]{0:T(1024)} %pad_clamp_fusion.1), kind=kCustom, calls=%fused_computation.3 | custom fusion | bytes 1572960 | tf_op jit(solution)/shard_map/gather | solution.py:42
  40.4 2.7 %gather_fusion.2 = bf16[36,64,256]{2,1,0:T(8,128)(2,1)} fusion(bf16[12,64,256]{2,1,0:T(8,128)(2,1)} %bitcast.8, s32[1024]{0:T(1024)S(1)} %pad_clamp_fusion.2), kind=kCustom, calls=%fused_computation.2 | custom fusion | bytes 2359440 | tf_op jit(solution)/shard_map/gather | solution.py:42
  43.1 2.7 %convolution_bitcast_fusion.4 = f32[12,256,64]{1,2,0:T(8,128)} fusion(bf16[12,16,64,64]{3,2,1,0:T(8,128)(2,1)S(1)} %reshape.42, bf16[12,3,64,256]{3,2,1,0:T(8,128)(2,1)} %bitcast.97, pred[12,3]{1,0:T(8,128)(4,1)S(1)} %copy-done.19), kind=kOutput, calls=%fused_computation.14 | convolution fusion | flops 76087296 | bytes 3538980 | tf_op jit(solution)/shard_map/rjab,rjbc->rac/dot_general | solution.py:50
  45.9 1.3 convolution_bitcast_fusion
  47.1 1.2 convolution_bitcast_fusion.2
  48.4 1.3 convolution_bitcast_fusion.6
  49.7 2.7 %gather_fusion.1 = bf16[36,64,256]{2,1,0:T(8,128)(2,1)} fusion(bf16[12,64,256]{2,1,0:T(8,128)(2,1)} %bitcast.4, s32[1024]{0:T(1024)S(1)} %pad_clamp_fusion.3), kind=kCustom, calls=%fused_computation.1 | custom fusion | bytes 2359440 | tf_op jit(solution)/shard_map/gather | solution.py:42
  52.4 2.3 %fusion.11 = f32[12,256,64]{1,2,0:T(8,128)S(1)} fusion(f32[12,256,64]{1,2,0:T(8,128)} %convolution_bitcast_fusion.4, f32[12,256,64]{1,2,0:T(8,128)} %fusion.2, bf16[12,16,64,64]{3,2,1,0:T(8,128)(2,1)S(1)} %reshape.42, bf16[12,3,64,256]{3,2,1,0:T(8,128)(2,1)} %bitcast.85, pred[12,3]{1,0:T(8,128)(4,1)S(1)} %copy-done.17), kind=kOutput, calls=%fused_computation.25 | convolution fusion | flops 76480512 | bytes 5111844 | tf_op jit(solution)/shard_map/rjab,rjbc->rac/dot_general | solution.py:50
  55.1 1.0 convolution_bitcast_fusion.8
  58.8 1.0 convolution_bitcast_fusion.9
  59.8 73.0 %all-reduce.5.cloned.1.call-done = (f32[256,256]{0,1:T(8,128)}, f32[256,256]{0,1:T(8,128)}) async-done(((f32[256,256]{0,1:T(8,128)}, f32[256,256]{0,1:T(8,128)}), (f32[256,256]{0,1:T(8,128)}, f32[256,256]{0,1:T(8,128)})) %all-reduce.5.cloned.1.call-update) | async-done | bytes 524304 | tf_op jit(solution)/shard_map/psum | solution.py:12
  132.9 34.9 %all-reduce.7.cloned.1.call-done = (f32[256,256]{0,1:T(8,128)}, f32[256,256]{0,1:T(8,128)}) async-done(((f32[256,256]{0,1:T(8,128)}, f32[256,256]{0,1:T(8,128)}), (f32[256,256]{0,1:T(8,128)}, f32[256,256]{0,1:T(8,128)})) %all-reduce.7.cloned.1.call-update) | async-done | bytes 524304 | tf_op jit(solution)/shard_map/psum | solution.py:13
  167.8 1.1 broadcast_multiply_fusion
  168.9 0.8 copy.11
  (66 shorter events, 8.8 us)
Async XLA Ops:
  7.2 125.7 %all-reduce.5.cloned.1.call-start = ((), (), s32[]{:S(2)}) async-start(), calls=%async_computation | async-start | bytes 1048576 | tf_op jit(solution)/shard_map/psum | solution.py:12
  7.2 33.2 %collective-permute-start.1 = (bf16[768,256]{1,0:T(8,128)(2,1)}, bf16[768,256]{1,0:T(8,128)(2,1)}, u32[]{:S(2)}, u32[]{:S(2)}) collective-permute-start(bf16[768,256]{1,0:T(8,128)(2,1)} %param.5), channel_id=1, source_target_pairs={{24,0},{0,8},{8,16},{16,24},{25,1},{1,9},{9,17},{17,25},{26,2},{2,... | collective-permute-start | bytes 1179656 | tf_op jit(solution)/shard_map/ppermute | solution.py:19
  7.7 42.0 %collective-permute-start = (bf16[768,256]{1,0:T(8,128)(2,1)}, bf16[768,256]{1,0:T(8,128)(2,1)}, u32[]{:S(2)}, u32[]{:S(2)}) collective-permute-start(bf16[768,256]{1,0:T(8,128)(2,1)} %param.5), channel_id=1, source_target_pairs={{8,0},{16,8},{24,16},{0,24},{9,1},{17,9},{25,17},{1,25},{10,2},{18... | collective-permute-start | bytes 1179656 | tf_op jit(solution)/shard_map/ppermute | solution.py:19
  9.7 25.5 %collective-permute-start.2 = (bf16[768,256]{1,0:T(8,128)(2,1)}, bf16[768,256]{1,0:T(8,128)(2,1)}, u32[]{:S(2)}, u32[]{:S(2)}) collective-permute-start(bf16[768,256]{1,0:T(8,128)(2,1)} %param.5), channel_id=1, source_target_pairs={{16,0},{24,8},{0,16},{8,24},{17,1},{25,9},{1,17},{9,25},{18,2},{26... | collective-permute-start | bytes 1179656 | tf_op jit(solution)/shard_map/ppermute | solution.py:19
  22.4 5.6 %copy-start = (bf16[768,256]{1,0:T(8,128)(2,1)S(1)}, bf16[768,256]{1,0:T(8,128)(2,1)}, u32[]{:S(2)}) copy-start(bf16[768,256]{1,0:T(8,128)(2,1)} %param.5) | copy-start | bytes 1179652
  30.3 3.4 %copy-start.1 = (bf16[12,16,64,64]{3,2,1,0:T(8,128)(2,1)S(1)}, bf16[12,16,64,64]{3,2,1,0:T(8,128)(2,1)}, u32[]{:S(2)}) copy-start(bf16[12,16,64,64]{3,2,1,0:T(8,128)(2,1)} %reshape.38) | copy-start | bytes 4718596
  30.3 3.4 %copy-start.9 = (bf16[72,64,256]{2,1,0:T(8,128)(2,1)S(1)}, bf16[72,64,256]{2,1,0:T(8,128)(2,1)}, u32[]{:S(2)}) copy-start(bf16[72,64,256]{2,1,0:T(8,128)(2,1)} %gather_fusion) | copy-start | bytes 7077892
  33.7 1.5 copy-start.15
  37.8 5.4 %copy-start.19 = (pred[12,3]{1,0:T(8,128)(4,1)S(1)}, pred[12,3]{1,0:T(8,128)(4,1)}, u32[]{:S(2)}) copy-start(pred[12,3]{1,0:T(8,128)(4,1)} %get-tuple-element.23) | copy-start | bytes 112
  40.4 5.5 %copy-start.18 = (pred[12,2]{1,0:T(8,128)(4,1)S(1)}, pred[12,2]{1,0:T(8,128)(4,1)}, u32[]{:S(2)}) copy-start(pred[12,2]{1,0:T(8,128)(4,1)} %get-tuple-element.21) | copy-start | bytes 76
  43.1 2.7 %copy-start.6 = (bf16[24,64,256]{2,1,0:T(8,128)(2,1)S(1)}, bf16[24,64,256]{2,1,0:T(8,128)(2,1)}, u32[]{:S(2)}) copy-start(bf16[24,64,256]{2,1,0:T(8,128)(2,1)} %gather_fusion.4) | copy-start | bytes 2359300
  43.1 4.0 %copy-start.2 = (bf16[12,16,64,64]{3,2,1,0:T(8,128)(2,1)S(1)}, bf16[12,16,64,64]{3,2,1,0:T(8,128)(2,1)}, u32[]{:S(2)}) copy-start(bf16[12,16,64,64]{3,2,1,0:T(8,128)(2,1)} %reshape.38) | copy-start | bytes 4718596
  45.9 2.5 %copy-start.12 = (bf16[36,64,256]{2,1,0:T(8,128)(2,1)S(1)}, bf16[36,64,256]{2,1,0:T(8,128)(2,1)}, u32[]{:S(2)}) copy-start(bf16[36,64,256]{2,1,0:T(8,128)(2,1)} %gather_fusion.2) | copy-start | bytes 3538948
  48.4 4.0 %copy-start.17 = (pred[12,3]{1,0:T(8,128)(4,1)S(1)}, pred[12,3]{1,0:T(8,128)(4,1)}, u32[]{:S(2)}) copy-start(pred[12,3]{1,0:T(8,128)(4,1)} %get-tuple-element.22) | copy-start | bytes 112
  52.4 2.3 %copy-start.5 = (bf16[24,64,256]{2,1,0:T(8,128)(2,1)S(1)}, bf16[24,64,256]{2,1,0:T(8,128)(2,1)}, u32[]{:S(2)}) copy-start(bf16[24,64,256]{2,1,0:T(8,128)(2,1)} %gather_fusion.3) | copy-start | bytes 2359300
  52.4 2.3 %copy-start.8 = (f32[12,256,64]{1,2,0:T(8,128)S(1)}, f32[12,256,64]{1,2,0:T(8,128)}, u32[]{:S(2)}) copy-start(f32[12,256,64]{1,2,0:T(8,128)} %convolution_bitcast_fusion) | copy-start | bytes 2359300
  52.4 2.4 %copy-start.16 = (pred[12,2]{1,0:T(8,128)(4,1)S(1)}, pred[12,2]{1,0:T(8,128)(4,1)}, u32[]{:S(2)}) copy-start(pred[12,2]{1,0:T(8,128)(4,1)} %get-tuple-element.20) | copy-start | bytes 76
  52.4 3.7 %copy-start.13 = (f32[12,256,64]{1,2,0:T(8,128)S(1)}, f32[12,256,64]{1,2,0:T(8,128)}, u32[]{:S(2)}) copy-start(f32[12,256,64]{1,2,0:T(8,128)} %fusion.3) | copy-start | bytes 2359300
  52.4 3.7 %copy-start.14 = (f32[12,256,64]{1,2,0:T(8,128)S(1)}, f32[12,256,64]{1,2,0:T(8,128)}, u32[]{:S(2)}) copy-start(f32[12,256,64]{1,2,0:T(8,128)} %convolution_bitcast_fusion.6) | copy-start | bytes 2359300
  54.7 2.2 %copy-start.3 = (bf16[12,16,64,64]{3,2,1,0:T(8,128)(2,1)S(1)}, bf16[12,16,64,64]{3,2,1,0:T(8,128)(2,1)}, u32[]{:S(2)}) copy-start(bf16[12,16,64,64]{3,2,1,0:T(8,128)(2,1)} %reshape.38) | copy-start | bytes 4718596
  54.7 2.5 %copy-start.4 = (bf16[36,64,256]{2,1,0:T(8,128)(2,1)S(1)}, bf16[36,64,256]{2,1,0:T(8,128)(2,1)}, u32[]{:S(2)}) copy-start(bf16[36,64,256]{2,1,0:T(8,128)(2,1)} %gather_fusion.1) | copy-start | bytes 3538948
  55.1 2.6 %copy-start.10 = (bf16[12,256,64]{1,2,0:T(8,128)(2,1)}, bf16[12,256,64]{1,2,0:T(8,128)(2,1)S(1)}, u32[]{:S(2)}) copy-start(bf16[12,256,64]{1,2,0:T(8,128)(2,1)S(1)} %fusion.12) | copy-start | bytes 1179652
  58.7 111.8 %copy-start.11 = (bf16[12,256,64]{1,2,0:T(8,128)(2,1)}, bf16[12,256,64]{1,2,0:T(8,128)(2,1)S(1)}, u32[]{:S(2)}) copy-start(bf16[12,256,64]{1,2,0:T(8,128)(2,1)S(1)} %fusion.13) | copy-start | bytes 1179652
  59.8 108.0 %all-reduce.7.cloned.1.call-start = ((), (), s32[]{:S(2)}) async-start(), calls=%async_computation.1 | async-start | bytes 1048576 | tf_op jit(solution)/shard_map/psum | solution.py:13
  (1 other events, 1.1 us)
Sparse Core Ops, SparseCore 0:
  59.9 72.9 all-reduce.4
  135.4 32.3 all-reduce.6
